TPU v7x, 32 devices: a whole 2x2x4 slice. The times are simulated.
32 devices in a mesh: view: 4 (over y, core), bx: 2 (over x), by: 4 (over z).
Axes of the slice: x: 2, y: 2, z: 4, core: 2. Of those that a mesh axis runs over, the one named last changes fastest.
Arguments:
- estimate: float32 [2048, 512], P(('bx', 'by')), may hold values from 0.5 to 2
- recorded: float32 [4, 2048, 512], P('view', ('bx', 'by')), may hold values from 0.5 to 4
- resample: float32 [4, 4, 512, 512], P('view'), may hold values from 0 to 1, as said below
- psf_taps: float32 [4, 31], P('view'), may hold values from 0.2 to 1
- source_brick: int32 [4, 2048, 4], P('view', ('bx', 'by')), may hold values from 0 to 7, all different within a row; in each aligned block of 256 rows (0 to 255, 256 to 511, ..., all dimensions but the last counted through in order) at most 192 rows name the same one
- source_column: int32 [4, 2048, 4], P('view', ('bx', 'by')), may hold values from 0 to 255
Outputs:
- refined: float32 [2048, 512], P(('bx', 'by'))
Inputs may be any that keep to these rules, and one draw needn't show every extreme that they name: `source_brick`: in each view, the 4 bricks named for one column are different; among the columns of one brick, no joined brick is named more than 192 times, and some joined brick exactly 192 times. `resample`: all entries are nonnegative.
All inputs are finite; a program needn't handle non-finite values.
Results may differ from a plain program's by a relative error of at most 0.0001.
Values sent between devices are 32-bit elements; how exact they have to be, the bound alone decides.
A program may use at most 192 MiB of HBM per device.

v0:
```python
import jax
import jax.numpy as jnp
from jax import lax
from jax.sharding import PartitionSpec as P

ITERS = 2


precise = lax.Precision.HIGHEST


def blur_matrix(taps_row, column_len):
    spread = taps_row / jnp.sum(taps_row)
    tap_count = spread.shape[0]
    half_width = (tap_count - 1) // 2
    row_ids = lax.broadcasted_iota(jnp.int32, (column_len, column_len), 0)
    col_ids = lax.broadcasted_iota(jnp.int32, (column_len, column_len), 1)
    offset = row_ids - col_ids + half_width
    matrix = jnp.zeros((column_len, column_len), jnp.float32)
    for tap_number in range(tap_count):
        matrix = matrix + jnp.where(offset == tap_number, spread[tap_number], 0.0)
    return matrix


def per_device(estimate, recorded, resample, psf_taps, source_brick, source_column):
    bricks_x = lax.axis_size("bx")
    bricks_y = lax.axis_size("by")
    peer_count = bricks_x * bricks_y
    columns, column_len = estimate.shape
    sources = source_brick.shape[2]
    pair_count = columns * sources
    capacity = 3 * pair_count // (2 * peer_count)
    peer_ids = source_brick[0].reshape(pair_count)
    wanted = source_column[0].reshape(pair_count)
    branch_ids = lax.broadcasted_iota(jnp.int32, (columns, sources), 1).reshape(pair_count)
    peer_hits = (
        peer_ids[:, None] == lax.broadcasted_iota(jnp.int32, (pair_count, peer_count), 1)
    ).astype(jnp.int32)
    before = jnp.cumsum(peer_hits, axis=0) - peer_hits
    slot_rank = jnp.sum(before * peer_hits, axis=1)
    position = peer_ids * capacity + slot_rank
    request = (
        jnp.full((peer_count * capacity,), -1, jnp.int32)
        .at[position]
        .set(wanted * sources + branch_ids)
    )
    served = lax.all_to_all(
        request.reshape(peer_count, capacity), ("bx", "by"), split_axis=0, concat_axis=0, tiled=True
    )
    served = served.reshape(peer_count * capacity)
    owned_column = jnp.maximum(served, 0) // sources
    weights = resample[0]
    blurring = blur_matrix(psf_taps[0], column_len)
    unit_smeared = jnp.sum(blurring, axis=1)
    unit_back = jnp.einsum("b,kcb->kc", unit_smeared, weights, precision=precise)
    normalizer = None
    norm_local = None
    for sweep in range(ITERS):
        outgoing = estimate[owned_column]
        incoming = lax.all_to_all(
            outgoing.reshape(peer_count, capacity, column_len),
            ("bx", "by"),
            split_axis=0,
            concat_axis=0,
            tiled=True,
        )
        incoming = incoming.reshape(peer_count * capacity, column_len)
        pieces = incoming[position].reshape(columns, sources, column_len)
        forward = jnp.einsum("qkb,kbc->qc", pieces, weights, precision=precise)
        blurred = jnp.dot(forward, blurring, precision=precise)
        quotient = recorded[0] / blurred
        smeared = jnp.dot(quotient, blurring.T, precision=precise)
        contributions = jnp.einsum("qb,kcb->qkc", smeared, weights, precision=precise).reshape(
            pair_count, column_len
        )
        with_units = sweep == 0
        if with_units:
            unit_rows = jnp.broadcast_to(unit_back[None], (columns, sources, column_len)).reshape(
                pair_count, column_len
            )
            stacked = jnp.stack([contributions, unit_rows], axis=1)
        else:
            stacked = contributions[:, None, :]
        layers = stacked.shape[1]
        buffer = (
            jnp.zeros((peer_count * capacity, layers, column_len), jnp.float32)
            .at[position]
            .set(stacked)
        )
        returned = lax.all_to_all(
            buffer.reshape(peer_count, capacity, layers, column_len),
            ("bx", "by"),
            split_axis=0,
            concat_axis=0,
            tiled=True,
        )
        returned = returned.reshape(peer_count * capacity, layers, column_len)
        owned_sum = (
            jnp.zeros((columns, layers, column_len), jnp.float32).at[owned_column].add(returned)
        )
        correction_local = owned_sum[:, 0]
        if with_units:
            norm_local = owned_sum[:, 1]
        if sweep == 0:
            summands = jnp.stack([correction_local, norm_local])
        else:
            summands = correction_local[None]
        view_total = lax.psum(summands, "view")
        if sweep == 0:
            normalizer = view_total[1]
        estimate = estimate * (view_total[0] + 1.0) / (normalizer + 1.0)
    return estimate


def solution(mesh):
    return jax.shard_map(
        per_device,
        mesh=mesh,
        in_specs=(
            P(("bx", "by"), None),
            P("view", ("bx", "by"), None),
            P("view", None, None, None),
            P("view", None),
            P("view", ("bx", "by"), None),
            P("view", ("bx", "by"), None),
        ),
        out_specs=P(("bx", "by"), None),
        check_vma=False,
    )
```

profile of v0, /device:TPU:0, one launch (start us, length us, event | category | flops | bytes accessed | tf_op | source)
XLA Modules:
  0.0 891.3 jit_solution(9087115394177621034)
XLA Ops:
  17.0 13.6 %all_to_all.29 = s32[8,1,192]{2,1,0:T(1,128)S(1)} all-to-all(s32[8,1,192]{2,1,0:T(1,128)S(1)} %all_to_all.18), channel_id=1, replica_groups=mesh['view'=4,'bx'=2,'by'=4] {'bx','by'}, dimensions={0} | all-to-all | bytes 12288 | tf_op jit(solution)/shard_map/all_to_all | solution.py:47
  30.8 5.0 gather_fusion
  43.2 22.8 %fusion.58 = f32[512]{0:T(512)S(1)} fusion(f32[]{:T(128)} %bitcast.38, f32[]{:T(128)} %bitcast.37, f32[]{:T(128)} %bitcast.36, f32[]{:T(128)} %bitcast.35, f32[]{:T(128)} %bitcast.34, f32[]{:T(128)} %bitcast.33, f32[]{:T(128)} %bitcast.32, f32[]{:T(128)} %bitcast.31, f32[]{:T(128)} %bitcast.30, f32[]{:T(128)} %bitcast.29, f32[]{:T(128)} %bitcast.28, ...), kind=kLoop, calls=%fused_computation.73 | loop fusion | flops 24903168 | bytes 2172 | tf_op jit(solution)/shard_map/reduce_sum | solution.py:54
  66.0 5.7 fusion.4
  73.7 37.0 %all-to-all-done.1 = f32[8,192,512]{2,1,0:T(8,128)} async-done(((f32[8,192,512]{2,1,0:T(8,128)}), f32[8,192,512]{2,1,0:T(8,128)}, u32[]{:S(2)}, u32[]{:S(2)}) %all-to-all-start.1) | async-done | bytes 3145760 | tf_op jit(solution)/shard_map/all_to_all | solution.py:60
  110.7 5.9 gather_fusion.1
  118.3 7.2 fusion.14
  125.6 24.4 %convolution_divide_fusion.1 = f32[256,512]{1,0:T(8,128)S(1)} fusion(f32[256,512]{1,0:T(8,128)S(1)} %fusion.14, f32[1,256,512]{2,1,0:T(8,128)S(1)} %copy-done.5, f32[]{:T(128)} %bitcast.38, f32[]{:T(128)} %bitcast.37, f32[]{:T(128)} %bitcast.36, f32[]{:T(128)} %bitcast.35, f32[]{:T(128)} %bitcast.34, f32[]{:T(128)} %bitcast.33, f32[]{:T(128)} %bitcast.32, ...), kind=kOutput, calls=%fused_computation.25 | convolution fusion | flops 830078976 | bytes 1572988 | tf_op jit(solution)/shard_map/dot_general | solution.py:70
  150.0 25.1 %convolution_bitcast_fusion.1 = f32[256,512,1]{1,0,2:T(8,128)S(1)} fusion(f32[256,512]{1,0:T(8,128)S(1)} %convolution_divide_fusion.1, f32[]{:T(128)} %bitcast.38, f32[]{:T(128)} %bitcast.37, f32[]{:T(128)} %bitcast.36, f32[]{:T(128)} %bitcast.35, f32[]{:T(128)} %bitcast.34, f32[]{:T(128)} %bitcast.33, f32[]{:T(128)} %bitcast.32, f32[]{:T(128)} %bitcast.31, ...), kind=kOutput, calls=%fused_computation.29 | convolution fusion | flops 829947904 | bytes 1048700 | tf_op jit(solution)/shard_map/dot_general | solution.py:72
  184.6 5.3 copy.45
  194.2 104.3 %scatter_fusion = f32[1536,2,512]{2,1,0:T(2,128)} fusion(f32[1536,2,512]{2,1,0:T(2,128)} %broadcast_in_dim.160, s32[1024]{0:T(1024)S(1)} %bitcast.129, f32[1024,2,512]{2,1,0:T(2,128)} %copy.45), kind=kCustom, calls=%fused_computation.5 | custom fusion | bytes 12587008 | tf_op jit(solution)/shard_map/scatter | solution.py:88
  298.5 142.2 %all_to_all.30 = f32[8,192,2,512]{3,2,1,0:T(2,128)} all-to-all(f32[8,192,2,512]{3,2,1,0:T(2,128)} %bitcast.120), channel_id=1, replica_groups=mesh['view'=4,'bx'=2,'by'=4] {'bx','by'}, dimensions={0} | all-to-all | bytes 12582912 | tf_op jit(solution)/shard_map/all_to_all | solution.py:90
  441.0 123.7 %scatter_fusion.1 = f32[256,2,512]{2,1,0:T(2,128)S(1)} fusion(f32[256,2,512]{2,1,0:T(2,128)S(1)} %broadcast_in_dim.158, s32[1536]{0:T(1024)S(1)} %fusion.67, f32[1536,2,512]{2,1,0:T(2,128)} %bitcast.121), kind=kCustom, calls=%fused_computation.6 | custom fusion | flops 1572864 | bytes 18880512 | tf_op jit(solution)/shard_map/scatter-add | solution.py:99
  567.6 33.4 %all-reduce.3.cloned.1.call-done = f32[2,256,512]{2,0,1:T(2,128)} async-done(((f32[2,256,512]{2,0,1:T(2,128)}), f32[2,256,512]{2,0,1:T(2,128)}) %all-reduce.3.cloned.1.call-update) | async-done | bytes 1048592 | tf_op jit(solution)/shard_map/psum | solution.py:108
  604.6 5.0 gather_fusion.2
  609.6 76.9 %all_to_all.31 = f32[8,192,512]{2,1,0:T(8,128)} all-to-all(f32[8,192,512]{2,1,0:T(8,128)} %bitcast.124), channel_id=1, replica_groups=mesh['view'=4,'bx'=2,'by'=4] {'bx','by'}, dimensions={0} | all-to-all | bytes 6291456 | tf_op jit(solution)/shard_map/all_to_all | solution.py:60
  686.5 5.9 gather_fusion.3
  694.1 7.2 fusion.19
  701.3 24.4 %convolution_divide_fusion = f32[256,512]{1,0:T(8,128)S(1)} fusion(f32[256,512]{1,0:T(8,128)S(1)} %fusion.19, f32[1,256,512]{2,1,0:T(8,128)S(1)} %copy-done.6, f32[]{:T(128)} %bitcast.38, f32[]{:T(128)} %bitcast.37, f32[]{:T(128)} %bitcast.36, f32[]{:T(128)} %bitcast.35, f32[]{:T(128)} %bitcast.34, f32[]{:T(128)} %bitcast.33, f32[]{:T(128)} %bitcast.32, ...), kind=kOutput, calls=%fused_computation.24 | convolution fusion | flops 830078976 | bytes 1572988 | tf_op jit(solution)/shard_map/dot_general | solution.py:70
  725.7 24.9 %convolution_bitcast_fusion = f32[256,512,1]{1,0,2:T(8,128)S(1)} fusion(f32[256,512]{1,0:T(8,128)S(1)} %convolution_divide_fusion, f32[]{:T(128)} %bitcast.38, f32[]{:T(128)} %bitcast.37, f32[]{:T(128)} %bitcast.36, f32[]{:T(128)} %bitcast.35, f32[]{:T(128)} %bitcast.34, f32[]{:T(128)} %bitcast.33, f32[]{:T(128)} %bitcast.32, f32[]{:T(128)} %bitcast.31, ...), kind=kOutput, calls=%fused_computation.28 | convolution fusion | flops 829947904 | bytes 1048700 | tf_op jit(solution)/shard_map/dot_general | solution.py:72
  757.5 7.3 scatter_custom_fusion.3
  764.7 74.6 %all_to_all.32 = f32[8,192,1,512]{3,1,2,0:T(8,128)} all-to-all(f32[8,192,1,512]{3,1,2,0:T(8,128)} %bitcast.122), channel_id=1, replica_groups=mesh['view'=4,'bx'=2,'by'=4] {'bx','by'}, dimensions={0} | all-to-all | bytes 6291456 | tf_op jit(solution)/shard_map/all_to_all | solution.py:90
  839.4 12.0 %scatter_custom_fusion.4 = f32[256,512]{1,0:T(8,128)} fusion(s32[1536]{0:T(1024)S(1)} %fusion.67, f32[1536,512]{1,0:T(8,128)} %bitcast.125, f32[]{:T(128)} %constant.37.clone.1), kind=kCustom, calls=%fused_computation.74 | custom fusion | flops 786432 | bytes 524800 | tf_op jit(solution)/shard_map/scatter-add | solution.py:99
  851.4 30.8 %all-reduce.5.cloned.1.call-done = f32[1,256,512]{2,1,0:T(8,128)} async-done(((f32[1,256,512]{2,1,0:T(8,128)}), f32[1,256,512]{2,1,0:T(8,128)}) %all-reduce.5.cloned.1.call-update) | async-done | bytes 524304 | tf_op jit(solution)/shard_map/psum | solution.py:108
  (72 shorter events, 52.8 us)
Async XLA Ops:
  6.5 24.2 %copy-start = (f32[256,512]{1,0:T(8,128)S(1)}, f32[256,512]{1,0:T(8,128)}, u32[]{:S(2)}) copy-start(f32[256,512]{1,0:T(8,128)} %param.6) | copy-start | bytes 1572868
  35.7 4.8 copy-start.7
  35.7 75.0 %all-to-all-start.1 = ((f32[8,192,512]{2,1,0:T(8,128)}), f32[8,192,512]{2,1,0:T(8,128)}, u32[]{:S(2)}, u32[]{:S(2)}) async-start(f32[8,192,512]{2,1,0:T(8,128)} %bitcast.123), calls=%async_computation.1 | async-start | bytes 6291456 | tf_op jit(solution)/shard_map/all_to_all | solution.py:60
  40.3 560.7 %all-reduce.3.cloned.1.call-start = ((), (), s32[]{:S(2)}) async-start(), calls=%async_computation.5 | async-start | bytes 2097152 | tf_op jit(solution)/shard_map/psum | solution.py:108
  118.3 7.2 copy-start.5
  150.0 25.1 %copy-start.1 = (f32[1,4,512,512]{3,2,1,0:T(8,128)S(1)}, f32[1,4,512,512]{3,2,1,0:T(8,128)}, u32[]{:S(2)}) copy-start(f32[1,4,512,512]{3,2,1,0:T(8,128)} %param.8) | copy-start | bytes 12582916
  567.6 314.6 %all-reduce.5.cloned.1.call-start = ((), (), s32[]{:S(2)}) async-start(), calls=%async_computation.6 | async-start | bytes 1048576 | tf_op jit(solution)/shard_map/psum | solution.py:108
  603.6 0.8 copy-start.3
  694.0 7.2 copy-start.6
  725.7 24.9 %copy-start.2 = (f32[1,4,512,512]{3,2,1,0:T(8,128)S(1)}, f32[1,4,512,512]{3,2,1,0:T(8,128)}, u32[]{:S(2)}) copy-start(f32[1,4,512,512]{3,2,1,0:T(8,128)} %param.8) | copy-start | bytes 12582916
  764.7 117.5 %copy-start.4 = (f32[1,256,512]{2,0,1:T(1,128)S(1)}, f32[1,256,512]{2,0,1:T(1,128)}, u32[]{:S(2)}) copy-start(f32[1,256,512]{2,0,1:T(1,128)} %copy-done.3) | copy-start | bytes 1572868
Sparse Core Ops, SparseCore 0:
  567.7 33.3 all-reduce.2
  851.5 30.6 all-reduce.4
where the time goes:
time: 903 us; the launch traced here: 891 us
  blocking collectives  307 us (34%)
  other arithmetic  173 us (19%)
  local copies, waits for them, and re-layouts  164 us (18%)
  matrix products  126 us (14%)
  waiting for transfers between devices  101 us (11%)
  between operations  14 us (2%)
    all_to_all x2, blocking collectives, per_device(): lax.all_to_all(buffer.reshape(peer_count, capacity, layers, column_len),...  217 us
    scatter-add x2, other arithmetic, per_device(): jnp.zeros((columns, layers, column_len), jnp.float32).at[owned_column]  136 us
    scatter x2, local copies, waits for them, and re-layouts, per_device(): buffer = jnp.zeros((peer_count * capacity, layers, column_len), jnp.float...  112 us
    all_to_all x1, blocking collectives, per_device(): lax.all_to_all(outgoing.reshape(peer_count, capacity, column_len), ('bx',...  76.9 us
    psum x2, waiting for transfers between devices, per_device(): view_total = lax.psum(summands, 'view')  64.2 us
    dot_general x2, matrix products, per_device(): smeared = jnp.dot(quotient, blurring.T, precision=precise)  49.9 us
    dot_general x2, matrix products, per_device(): blurred = jnp.dot(forward, blurring, precision=precise)  48.8 us
    all_to_all x1, waiting for transfers between devices, per_device(): lax.all_to_all(outgoing.reshape(peer_count, capacity, column_len), ('bx',...  37 us
  transfers between devices with their start and end apart: 3, of which 3 were waited for; matrix products, arithmetic and copies ran while one was open for 4% of the time, Pallas kernels for 0%

commit v1 on v0

v1 whole, which is shorter than its diff:
```python
import functools

import jax
import jax.numpy as jnp
from jax import lax
from jax.experimental import pallas as pl
from jax.experimental.pallas import tpu as pltpu
from jax.sharding import PartitionSpec as P

ITERS = 2
F32 = jnp.float32
BF16 = jnp.bfloat16
VMEM = pltpu.VMEM
MESH = pl.DeviceIdType.MESH


def split(x):
    hi = x.astype(BF16)
    return hi, (x - hi.astype(F32)).astype(BF16)


def dot(a, b):
    return jnp.dot(a, b, preferred_element_type=F32)


def dot3(ah, al, bh, bl):
    return dot(ah, bh) + (dot(ah, bl) + dot(al, bh))


def prep_kernel(taps_ref, r_ref, bh, bl, bth, btl, rh, rl, rth, rtl, unit_ref):
    tap_count = taps_ref.shape[1]
    half = (tap_count - 1) // 2
    depth = bh.shape[0]
    total = taps_ref[0, 0]
    for t in range(1, tap_count):
        total = total + taps_ref[0, t]
    scale = 1.0 / jnp.full((1, depth), total, F32)
    offset = lax.broadcasted_iota(jnp.int32, (depth, depth), 0) - lax.broadcasted_iota(
        jnp.int32, (depth, depth), 1
    ) + half
    blur = jnp.zeros((depth, depth), F32)
    for t in range(tap_count):
        blur = jnp.where(offset == t, taps_ref[0, t], blur)
    blur = blur * scale
    bh[...], bl[...] = split(blur)
    bth[...], btl[...] = split(blur.T)
    smeared = jnp.sum(blur, axis=1, keepdims=True)
    for k in range(r_ref.shape[0]):
        w = r_ref[k]
        rh[k], rl[k] = split(w)
        wt = w.T
        rth[k], rtl[k] = split(wt)
        unit_ref[k : k + 1, :] = jnp.sum(wt * smeared, axis=0, keepdims=True)


def prep(taps, weights):
    sources, depth, _ = weights.shape
    flat = jax.ShapeDtypeStruct((depth, depth), BF16)
    cube = jax.ShapeDtypeStruct((sources, depth, depth), BF16)
    return pl.pallas_call(
        prep_kernel,
        out_shape=[flat] * 4 + [cube] * 4 + [jax.ShapeDtypeStruct((sources, depth), F32)],
        in_specs=[pl.BlockSpec(memory_space=pltpu.SMEM), pl.BlockSpec(memory_space=VMEM)],
        out_specs=[pl.BlockSpec(memory_space=VMEM)] * 9,
        compiler_params=pltpu.CompilerParams(vmem_limit_bytes=40 << 20),
        name="prep",
    )(taps, weights)


def sweep_kernel(
    field, ids_col, ids_row, recorded, bh, bl, bth, btl, rh, rl, rth, rtl, out, gh, gl, ch, cl
):
    total, depth = field.shape
    columns, sources = ids_col.shape
    chunk = min(total, 2048)
    lanes = lax.broadcasted_iota(jnp.int32, (columns, chunk), 1)
    for part in range(total // chunk):
        hi, lo = split(field[part * chunk : (part + 1) * chunk, :])
        for k in range(sources):
            rows = slice(k * columns, (k + 1) * columns)
            pick = jnp.where(ids_col[:, k : k + 1] - part * chunk == lanes, 1.0, 0.0).astype(BF16)
            ph = dot(pick, hi).astype(BF16)
            pm = dot(pick, lo).astype(BF16)
            if part == 0:
                gh[rows, :] = ph
                gl[rows, :] = pm
            else:
                gh[rows, :] = gh[rows, :] + ph
                gl[rows, :] = gl[rows, :] + pm
    forward = jnp.zeros((columns, depth), F32)
    for k in range(sources):
        rows = slice(k * columns, (k + 1) * columns)
        forward = forward + dot3(gh[rows, :], gl[rows, :], rh[k], rl[k])
    fh, fl = split(forward)
    qh, ql = split(recorded[...] / dot3(fh, fl, bh[...], bl[...]))
    sh, sl = split(dot3(qh, ql, bth[...], btl[...]))
    for k in range(sources):
        rows = slice(k * columns, (k + 1) * columns)
        ch[rows, :], cl[rows, :] = split(dot3(sh, sl, rth[k], rtl[k]))
    step = 256
    sub = lax.broadcasted_iota(jnp.int32, (step, columns * sources), 0)

    def scatter(s, carry):
        at = pl.multiple_of(s * step, step)
        put = jnp.where(ids_row[...] - at == sub, 1.0, 0.0).astype(BF16)
        out[pl.ds(at, step), :] = dot(put, ch[...]) + dot(put, cl[...])
        return carry

    lax.fori_loop(0, total // step, scatter, 0)


def run_sweep(field, ids_col, ids_row, recorded, mats):
    total, depth = field.shape
    columns, sources = ids_col.shape
    return pl.pallas_call(
        sweep_kernel,
        out_shape=jax.ShapeDtypeStruct((total, depth), F32),
        in_specs=[pl.BlockSpec(memory_space=VMEM)] * 12,
        out_specs=pl.BlockSpec(memory_space=VMEM),
        scratch_shapes=[pltpu.VMEM((columns * sources, depth), BF16)] * 4,
        compiler_params=pltpu.CompilerParams(vmem_limit_bytes=60 << 20),
        name="sweep",
    )(field, ids_col, ids_row, recorded, *mats)


def gather_stage(mine, field, x, z, v, mate, parity, sizes, sems):
    nx, nz, columns = sizes
    half = columns // 2
    zs, zr, xs, xr, ms, mr, local = sems

    def rows(dx, dz, p):
        brick = lax.rem(x - dx + nx, nx) * nz + lax.rem(z - dz + nz, nz)
        return field.at[pl.ds(pl.multiple_of(brick * columns + p * half, half), half), :]

    keep = pltpu.make_async_copy(mine, rows(0, 0, parity), local)
    keep.start()
    sends = []

    def send(src, dx, dz, s, r, to):
        copy = pltpu.make_async_remote_copy(
            src_ref=src, dst_ref=rows(dx, dz, parity), send_sem=s, recv_sem=r,
            device_id=to, device_id_type=MESH,
        )
        copy.start()
        sends.append(copy)

    def landed(dx, dz, p, s, r, to):
        pltpu.make_async_remote_copy(
            src_ref=mine, dst_ref=rows(dx, dz, p), send_sem=s, recv_sem=r,
            device_id=to, device_id_type=MESH,
        ).wait_recv()

    def to_x(src, dz):
        for dx in range(1, nx):
            send(src, 0, dz, xs.at[dx, dz], xr.at[dx, dz], {"bx": lax.rem(x + dx, nx)})

    to_x(mine, 0)
    for dz in range(nz - 1, 0, -1):
        send(mine, 0, 0, zs.at[dz], zr.at[dz], {"by": lax.rem(z + dz, nz)})
    send(mine, 0, 0, ms.at[0, 0], mr.at[0, 0], {"view": mate})
    for dz in range(1, nz):
        landed(0, dz, parity, zs.at[dz], zr.at[dz], {"by": z})
        to_x(rows(0, dz, parity), dz)
        send(rows(0, dz, parity), 0, dz, ms.at[0, dz], mr.at[0, dz], {"view": mate})
    for dz in range(nz):
        for dx in range(1, nx):
            landed(dx, dz, parity, xs.at[dx, dz], xr.at[dx, dz], {"bx": x})
            send(rows(dx, dz, parity), dx, dz, ms.at[dx, dz], mr.at[dx, dz], {"view": mate})
    for dz in range(nz):
        for dx in range(nx):
            landed(dx, dz, 1 - parity, ms.at[dx, dz], mr.at[dx, dz], {"view": mate})
    for copy in sends:
        copy.wait_send()
    keep.wait()


def scatter_stage(partial, own, x, z, v, mate, parity, sizes, bufs, sems):
    nx, nz, columns = sizes
    half = columns // 2
    nv = lax.axis_size("view")
    mbuf, xbuf, zbuf, ybuf = bufs
    zs, zr, xs, xr, ms, mr, ys, yr = sems

    def rows(dx, dz, p):
        brick = lax.rem(x + dx, nx) * nz + lax.rem(z + dz, nz)
        return pl.ds(pl.multiple_of(brick * columns + p * half, half), half)

    sends = []

    def send(src, dst, s, r, to):
        copy = pltpu.make_async_remote_copy(
            src_ref=src, dst_ref=dst, send_sem=s, recv_sem=r, device_id=to, device_id_type=MESH
        )
        copy.start()
        sends.append(copy)
        return copy

    order_z = list(range(1, nz)) + [0]
    from_mate = {}
    for dx in list(range(1, nx)) + [0]:
        for dz in order_z:
            from_mate[dx, dz] = send(
                partial.at[rows(dx, dz, 1 - parity), :], mbuf.at[dx, dz],
                ms.at[dx, dz], mr.at[dx, dz], {"view": mate},
            )
    from_x = {}
    for dx in range(1, nx):
        for dz in order_z:
            from_mate[dx, dz].wait_recv()
            mbuf[dx, dz] = mbuf[dx, dz] + partial[rows(dx, dz, parity), :]
            from_x[dx, dz] = send(
                mbuf.at[dx, dz], xbuf.at[dx, dz], xs.at[dx, dz], xr.at[dx, dz],
                {"bx": lax.rem(x + dx, nx)},
            )
    from_z = {}
    for dz in order_z:
        from_mate[0, dz].wait_recv()
        acc = mbuf[0, dz] + partial[rows(0, dz, parity), :]
        for dx in range(1, nx):
            from_x[dx, dz].wait_recv()
            acc = acc + xbuf[dx, dz]
        if dz == 0:
            own[...] = acc
        else:
            mbuf[0, dz] = acc
            from_z[dz] = send(
                mbuf.at[0, dz], zbuf.at[dz], zs.at[dz], zr.at[dz], {"by": lax.rem(z + dz, nz)}
            )
    for dz in range(1, nz):
        from_z[dz].wait_recv()
        own[...] = own[...] + zbuf[dz]
    from_y = {}
    for j in range(1, nv // 2):
        from_y[j] = send(
            own, ybuf.at[j], ys.at[j], yr.at[j], {"view": lax.rem(v + 2 * j, nv)}
        )
    total = own[...]
    for j in range(1, nv // 2):
        from_y[j].wait_recv()
        total = total + ybuf[j]
    for copy in sends:
        copy.wait_send()
    return total


def where_am_i():
    nx, nz = lax.axis_size("bx"), lax.axis_size("by")
    x, z, v = lax.axis_index("bx"), lax.axis_index("by"), lax.axis_index("view")
    parity = lax.rem(v, 2)
    return nx, nz, x, z, v, v + 1 - 2 * parity, parity


def greet(nx, nz, x, z, v, mate, with_y):
    barrier = pltpu.get_barrier_semaphore()
    peers = [{"by": lax.rem(z + d, nz)} for d in range(1, nz)]
    peers += [{"bx": lax.rem(x + d, nx)} for d in range(1, nx)]
    peers += [{"view": mate}]
    nv = lax.axis_size("view")
    if with_y:
        peers += [{"view": lax.rem(v + 2 * j, nv)} for j in range(1, nv // 2)]
    for peer in peers:
        pl.semaphore_signal(barrier, inc=1, device_id=peer, device_id_type=MESH)
    pl.semaphore_wait(barrier, len(peers))


def first_kernel(est, field, *sems):
    nx, nz, x, z, v, mate, parity = where_am_i()
    columns = est.shape[0]
    half = columns // 2
    greet(nx, nz, x, z, v, mate, False)
    mine = est.at[pl.ds(pl.multiple_of(parity * half, half), half), :]
    gather_stage(mine, field, x, z, v, mate, parity, (nx, nz, columns), sems)


def update(est, norm, total, parity):
    half = est.shape[0] // 2
    at = pl.ds(pl.multiple_of(parity * half, half), half)
    return est[at, :] * (total + 1.0) / (norm[at, :] + 1.0)


def middle_kernel(partial, est, norm, field, mine, own, *rest):
    nx, nz, x, z, v, mate, parity = where_am_i()
    columns = est.shape[0]
    bufs, sems = rest[:4], rest[4:]
    greet(nx, nz, x, z, v, mate, True)
    sizes = (nx, nz, columns)
    total = scatter_stage(partial, own, x, z, v, mate, parity, sizes, bufs, sems[:8])
    mine[...] = update(est, norm, total, parity)
    gather_stage(mine, field, x, z, v, mate, parity, sizes, sems[8:])


def last_kernel(partial, est, norm, out, own, *rest):
    nx, nz, x, z, v, mate, parity = where_am_i()
    columns = est.shape[0]
    half = columns // 2
    bufs, sems = rest[:4], rest[4:]
    greet(nx, nz, x, z, v, mate, True)
    sizes = (nx, nz, columns)
    total = scatter_stage(partial, own, x, z, v, mate, parity, sizes, bufs, sems[:8])
    at = pl.ds(pl.multiple_of(parity * half, half), half)
    out[at, :] = update(est, norm, total, parity)
    copy = pltpu.make_async_remote_copy(
        src_ref=out.at[at, :], dst_ref=out.at[at, :], send_sem=sems[8], recv_sem=sems[9],
        device_id={"view": mate}, device_id_type=MESH,
    )
    copy.start()
    copy.wait()


def gather_sems(nx, nz):
    dma = pltpu.SemaphoreType.DMA
    return [dma((nz,)), dma((nz,))] + [dma((nx, nz))] * 4 + [dma]


def scatter_scratch(nx, nz, nv, half, depth):
    dma = pltpu.SemaphoreType.DMA
    bufs = [pltpu.VMEM((nx, nz, half, depth), F32)] * 2
    bufs += [pltpu.VMEM((nz, half, depth), F32), pltpu.VMEM((nv // 2, half, depth), F32)]
    return bufs + [dma((nz,)), dma((nz,))] + [dma((nx, nz))] * 4 + [dma((nv // 2,))] * 2


def params(number, vmem=48 << 20):
    return pltpu.CompilerParams(
        collective_id=number, has_side_effects=True, vmem_limit_bytes=vmem
    )


def per_device(estimate, recorded, resample, psf_taps, source_brick, source_column):
    nx, nz, nv = lax.axis_size("bx"), lax.axis_size("by"), lax.axis_size("view")
    columns, depth = estimate.shape
    sources = source_brick.shape[2]
    total = columns * nx * nz
    half = columns // 2
    ids = source_brick[0] * columns + source_column[0]
    ids_turned = ids.T
    ids_row = ids_turned.reshape(1, columns * sources)
    vm, hbm = pl.BlockSpec(memory_space=VMEM), pl.BlockSpec(memory_space=pl.ANY)
    whole = jax.ShapeDtypeStruct((total, depth), F32)
    *mats, unit = prep(psf_taps, resample[0])
    parts = lax.all_gather(ids_turned, ("view", "bx", "by"))
    units = lax.all_gather(unit, "view").reshape(nv * sources, depth)
    field = pl.pallas_call(
        first_kernel,
        out_shape=whole,
        in_specs=[vm],
        out_specs=hbm,
        scratch_shapes=gather_sems(nx, nz),
        compiler_params=params(1),
        name="spread_first",
    )(estimate)
    brick = lax.axis_index("bx") * nz + lax.axis_index("by")
    parts = parts.reshape(nv, nx * nz, sources, columns).transpose(0, 2, 1, 3)
    parts = parts.reshape(nv * sources, total, 1) - brick * columns
    owned = lax.broadcasted_iota(jnp.int32, (1, 1, columns), 2)
    counts = jnp.sum((parts == owned).astype(F32), axis=1)
    norm = jnp.einsum("nc,nd->cd", counts, units, precision=lax.Precision.HIGHEST)
    for turn in range(ITERS):
        partial = run_sweep(field, ids, ids_row, recorded[0], mats)
        scratch = [pltpu.VMEM((half, depth), F32)] + scatter_scratch(nx, nz, nv, half, depth)
        dma = pltpu.SemaphoreType.DMA
        if turn < ITERS - 1:
            field, mine = pl.pallas_call(
                middle_kernel,
                out_shape=[whole, jax.ShapeDtypeStruct((half, depth), F32)],
                in_specs=[vm] * 3,
                out_specs=[hbm, vm],
                scratch_shapes=scratch + gather_sems(nx, nz),
                compiler_params=params(2 + turn),
                name="fold_spread",
            )(partial, estimate, norm)
            estimate = lax.dynamic_slice_in_dim(field, brick * columns, columns, 0)
        else:
            estimate = pl.pallas_call(
                last_kernel,
                out_shape=jax.ShapeDtypeStruct((columns, depth), F32),
                in_specs=[vm] * 3,
                out_specs=vm,
                scratch_shapes=scratch + [dma, dma],
                compiler_params=params(2 + turn),
                name="fold_last",
            )(partial, estimate, norm)
    return estimate


def solution(mesh):
    return jax.shard_map(
        per_device,
        mesh=mesh,
        in_specs=(
            P(("bx", "by"), None),
            P("view", ("bx", "by"), None),
            P("view", None, None, None),
            P("view", None),
            P("view", ("bx", "by"), None),
            P("view", ("bx", "by"), None),
        ),
        out_specs=P(("bx", "by"), None),
        check_vma=False,
    )
```

time: 903 us -> 321 us (0.36); the launches traced: 891 us -> 319 us
  blocking collectives: 307 us -> 76.1 us
  Pallas kernels: 0 us -> 217 us
  other arithmetic: 173 us -> 6.46 us
  local copies, waits for them, and re-layouts: 164 us -> 18.5 us
  matrix products: 126 us -> 0.62 us
  waiting for transfers between devices: 101 us -> 0 us
  between operations: 14 us -> 0.15 us
    all_to_all x4 -> x0, blocking collectives: 307 us -> none  [the longest x2 217 us: per_device(): lax.all_to_all(buffer.reshape(peer_count, capacity, layers, column_len),...]
    pallas_call x0 -> x6, Pallas kernels: none -> 217 us  [the longest x1 87.5 us: per_device(): pl.pallas_call(middle_kernel, out_shape=[whole, jax.ShapeDtypeStruct((hal...]
    scatter-add x2 -> x0, other arithmetic: 136 us -> none  [per_device(): jnp.zeros((columns, layers, column_len), jnp.float32).at[owned_column]]
    dot_general x9 -> x1, matrix products: 126 us -> 0.62 us  [per_device(): jnp.einsum('nc,nd->cd', counts, units, precision=lax.Precision.HIGHEST)]
    scatter x3 -> x0, local copies, waits for them, and re-layouts: 116 us -> none  [the longest x2 112 us: per_device(): buffer = jnp.zeros((peer_count * capacity, layers, column_len), jnp.float...]
    all_gather x0 -> x2, blocking collectives: none -> 76.1 us  [the longest x1 70.8 us: per_device(): parts = lax.all_gather(ids_turned, ('view', 'bx', 'by'))]
    psum x2 -> x0, waiting for transfers between devices: 64.2 us -> none  [per_device(): view_total = lax.psum(summands, 'view')]
    all_to_all x1 -> x0, waiting for transfers between devices: 37 us -> none  [per_device(): lax.all_to_all(outgoing.reshape(peer_count, capacity, column_len), ('bx',...]
  transfers between devices with their start and end apart: 3 -> 0, of which waited for: 3 -> 0; matrix products, arithmetic and copies ran while one was open for 4% -> 0% of each run, Pallas kernels for 0% -> 0%
where the time goes in v1:
time: 321 us; the launch traced here: 319 us
  Pallas kernels  217 us (68%)
  blocking collectives  76.1 us (24%)
  local copies, waits for them, and re-layouts  18.5 us (6%)
  other arithmetic  6.46 us (2%)
    pallas_call x1, Pallas kernels, per_device(): pl.pallas_call(middle_kernel, out_shape=[whole, jax.ShapeDtypeStruct((hal...  87.5 us
    all_gather x1, blocking collectives, per_device(): parts = lax.all_gather(ids_turned, ('view', 'bx', 'by'))  70.8 us
    pallas_call x1, Pallas kernels, per_device(): pl.pallas_call(last_kernel, out_shape=jax.ShapeDtypeStruct((columns, dept...  46.9 us
    pallas_call x2, Pallas kernels, run_sweep(): pl.pallas_call(sweep_kernel, out_shape=jax.ShapeDtypeStruct((total, depth...  44 us
    pallas_call x1, Pallas kernels, per_device(): pl.pallas_call(first_kernel, out_shape=whole, in_specs=[vm], out_specs=hb...  34.3 us
    unnamed x35, local copies, waits for them, and re-layouts  17.2 us

profile of v1, /device:TPU:0, one launch (start us, length us, event | category | flops | bytes accessed | tf_op | source)
XLA Modules:
  0.0 319.4 jit_solution(6437639137849557707)
XLA Ops:
  0.0 0.7 multiply_add_fusion
  1.6 70.8 %all-gather.2 = s32[32,4,256]{2,1,0:T(4,128)S(1)} all-gather(s32[1,4,256]{2,1,0:T(4,128)S(1)} %copy.30), channel_id=2, replica_groups=mesh['view'=4,'bx'=2,'by'=4] {'view','bx','by'}, dimensions={0}, use_global_device_ids=true | all-gather | bytes 135168 | tf_op jit(solution)/shard_map/all_gather | solution.py:340
  72.5 5.7 %convert_reduce_fusion = f32[16,256]{1,0:T(8,128)S(1)} fusion(s32[16,2048]{1,0:T(8,128)S(1)} %bitcast.31), kind=kLoop, calls=%fused_computation | loop fusion | flops 25161728 | bytes 147456 | tf_op jit(solution)/shard_map/reduce_sum | solution.py:355
  78.2 1.0 copy-done.7
  79.3 34.3 %spread_first.1.field = f32[2048,512]{1,0:T(8,128)S(1)} custom-call(f32[256,512]{1,0:T(8,128)S(1)} %copy-done.7), custom_call_target="tpu_custom_call" | custom-call | tf_op jit(solution)/shard_map/spread_first/pallas_call | solution.py:342
  113.6 1.9 copy-done.1
  115.6 4.8 %prep.1 = (bf16[512,512]{1,0:T(8,128)(2,1)S(1)}, bf16[512,512]{1,0:T(8,128)(2,1)S(1)}, bf16[512,512]{1,0:T(8,128)(2,1)S(1)}, bf16[512,512]{1,0:T(8,128)(2,1)S(1)...) custom-call(f32[1,31]{1,0:T(1,128)S(1)} %copy-done.13, ...), custom_call_target="tpu_custom_call" | custom-call | tf_op jit(solution)/shard_map/prep/pallas_call | solution.py:60
  120.3 1.4 copy-done.2
  121.7 1.3 copy-done.3
  123.0 1.3 copy-done.4
  124.4 1.3 copy-done.5
  125.7 0.8 copy-done.9
  126.5 0.8 copy-done.10
  127.3 0.8 copy-done.11
  128.1 0.8 copy-done.12
  128.9 22.0 %sweep.2.partial = f32[2048,512]{1,0:T(8,128)} custom-call(f32[2048,512]{1,0:T(8,128)} %copy-done.1, s32[256,4]{1,0:T(8,128)} %bitcast.24, s32[1,1024]{1,0:T(1,128)} %bitcast.32, f32[256,512]{1,0:T(8,128)} %bitcast.26, bf16[512,512]{1,0:T(8,128)(2,1)} %copy-done.9, bf16[512,512]{1,0:T(8,128)(2,1)} %copy-done.10, bf16[512,512]{1,0:T(8,128)(2,1)} %copy-done.11, ...), custom_call_target="tpu_custom_call" | custom-call | tf_op jit(solution)/shard_map/sweep/pallas_call | solution.py:115
  150.9 5.4 %all-gather.3 = f32[4,4,512]{2,1,0:T(4,128)S(1)} all-gather(f32[1,4,512]{2,1,0:T(4,128)S(1)} %bitcast.20), channel_id=3, replica_groups=mesh['view'=4,'bx'=2,'by'=4] {'view'}, dimensions={0}, use_global_device_ids=true | all-gather | bytes 40960 | tf_op jit(solution)/shard_map/all_gather | solution.py:341
  156.9 87.5 %fold_spread.1 = (f32[2048,512]{1,0:T(8,128)S(1)}, f32[128,512]{1,0:T(8,128)}) custom-call(f32[2048,512]{1,0:T(8,128)} %sweep.2.partial, f32[256,512]{1,0:T(8,128)S(1)} %copy-done.8, f32[256,512]{1,0:T(8,128)S(1)} %fusion.norm), custom_call_target="tpu_custom_call" | custom-call | tf_op jit(solution)/shard_map/fold_spread/pallas_call | solution.py:362
  244.4 1.9 copy-done.6
  246.4 22.0 %sweep.3.partial = f32[2048,512]{1,0:T(8,128)} custom-call(f32[2048,512]{1,0:T(8,128)} %copy-done.6, s32[256,4]{1,0:T(8,128)} %bitcast.25, s32[1,1024]{1,0:T(1,128)} %bitcast.33, f32[256,512]{1,0:T(8,128)} %bitcast.27, bf16[512,512]{1,0:T(8,128)(2,1)} %copy-done.9, bf16[512,512]{1,0:T(8,128)(2,1)} %copy-done.10, bf16[512,512]{1,0:T(8,128)(2,1)} %copy-done.11, ...), custom_call_target="tpu_custom_call" | custom-call | tf_op jit(solution)/shard_map/sweep/pallas_call | solution.py:115
  268.4 1.1 constant_dynamic-slice_fusion.est
  269.4 2.2 copy-done
  271.6 46.9 %fold_last.1 = f32[256,512]{1,0:T(8,128)S(1)} custom-call(f32[2048,512]{1,0:T(8,128)S(1)} %copy-done, f32[256,512]{1,0:T(8,128)S(1)} %constant_dynamic-slice_fusion.est, f32[256,512]{1,0:T(8,128)S(1)} %fusion.norm), custom_call_target="tpu_custom_call" | custom-call | tf_op jit(solution)/shard_map/fold_last/pallas_call | solution.py:373
  318.6 0.8 copy.35
  (27 shorter events, 1.6 us)
Async XLA Ops:
  0.0 115.6 %copy-start.13 = (f32[1,31]{1,0:T(1,128)S(1)}, f32[1,31]{1,0:T(1,128)}, u32[]{:S(2)}) copy-start(f32[1,31]{1,0:T(1,128)} %taps_ref.1) | copy-start | bytes 376
  0.9 119.5 %copy-start.14 = (s32[1,256,4]{2,1,0:T(8,128)}, s32[1,256,4]{2,1,0:T(8,128)S(1)}, u32[]{:S(2)}) copy-start(s32[1,256,4]{2,1,0:T(8,128)S(1)} %copy.28) | copy-start | bytes 12292
  78.2 1.0 copy-start.7
  113.6 1.9 copy-start.1
  120.3 1.4 copy-start.2
  121.7 1.3 copy-start.3
  123.0 1.3 copy-start.4
  124.4 1.3 copy-start.5
  125.7 0.8 copy-start.9
  126.5 0.8 copy-start.10
  127.3 0.8 copy-start.11
  128.1 0.8 copy-start.12
  128.9 28.0 %copy-start.8 = (f32[256,512]{1,0:T(8,128)S(1)}, f32[256,512]{1,0:T(8,128)}, u32[]{:S(2)}) copy-start(f32[256,512]{1,0:T(8,128)} %est.3) | copy-start | bytes 1572868
  244.4 1.9 copy-start.6
  269.4 2.2 copy-start

commit v2 on v0

v2 whole, which is shorter than its diff:
```python
import jax
import jax.numpy as jnp
from jax import lax
from jax.experimental import pallas as pl
from jax.experimental.pallas import tpu as pltpu
from jax.sharding import PartitionSpec as P

ITERS = 2
F32 = jnp.float32
BF16 = jnp.bfloat16
VMEM = pltpu.VMEM
MESH = pl.DeviceIdType.MESH


def split(x):
    hi = x.astype(BF16)
    return hi, (x - hi.astype(F32)).astype(BF16)


def dot(a, b):
    return jnp.dot(a, b, preferred_element_type=F32)


def dot3(ah, al, bh, bl):
    return dot(ah, bh) + (dot(ah, bl) + dot(al, bh))


def prep_stage(taps_ref, r_ref, bh, bl, bth, btl, rh, rl, rth, rtl, unit):
    tap_count = taps_ref.shape[1]
    half = (tap_count - 1) // 2
    depth = bh.shape[0]
    total = taps_ref[0, 0]
    for t in range(1, tap_count):
        total = total + taps_ref[0, t]
    scale = 1.0 / jnp.full((1, depth), total, F32)
    offset = lax.broadcasted_iota(jnp.int32, (depth, depth), 0) - lax.broadcasted_iota(
        jnp.int32, (depth, depth), 1
    ) + half
    blur = jnp.zeros((depth, depth), F32)
    for t in range(tap_count):
        blur = jnp.where(offset == t, taps_ref[0, t], blur)
    blur = blur * scale
    bh[...], bl[...] = split(blur)
    bth[...], btl[...] = split(blur.T)
    smeared = jnp.sum(blur, axis=1, keepdims=True)
    for k in range(r_ref.shape[0]):
        w = r_ref[k]
        rh[k], rl[k] = split(w)
        wt = w.T
        rth[k], rtl[k] = split(wt)
        unit[k : k + 1, :] = jnp.sum(wt * smeared, axis=0, keepdims=True)


def kernel(
    taps, r_ref, est, recorded, ids_col, ids_row, ids_turned, out, *rest
):
    (
        field, stage, mine, own, my_count, my_unit, norm, partial, mbuf, xbuf, zbuf, ybuf, idsbuf, cnt, units,
        bh, bl, bth, btl, rh, rl, rth, rtl, acc, ch, cl, th, tl, id_cols,
        gz, gx, gm, fz, fx, fm, fy, isem, csem, usem, osem, local,
    ) = rest
    in_vmem = stage.shape[0] == 8
    nx, nz, nv = lax.axis_size("bx"), lax.axis_size("by"), lax.axis_size("view")
    x, z, v = lax.axis_index("bx"), lax.axis_index("by"), lax.axis_index("view")
    parity = lax.rem(v, 2)
    mate = v + 1 - 2 * parity
    columns, depth = est.shape
    half = columns // 2
    sources = ids_col.shape[1]
    pairs = columns * sources

    def peer_x(d):
        return {"bx": lax.rem(x + d, nx)}

    def peer_z(d):
        return {"by": lax.rem(z + d, nz)}

    def peer_v(d):
        return {"view": lax.rem(v + d, nv)}

    def peer_xz(dx, dz):
        return {"bx": lax.rem(x + dx, nx), "by": lax.rem(z + dz, nz)}

    at_half = pl.ds(pl.multiple_of(parity * half, half), half)
    others = [(dx, dz) for dx in range(nx) for dz in range(nz) if dx or dz]
    barrier = pltpu.get_barrier_semaphore()
    peers = [peer_xz(dx, dz) for dx, dz in others] + [peer_v(d) for d in range(1, nv)]
    for peer in peers:
        pl.semaphore_signal(barrier, inc=1, device_id=peer, device_id_type=MESH)
    pl.semaphore_wait(barrier, len(peers))

    def remote(src, dst, sems, at, to):
        return pltpu.make_async_remote_copy(
            src_ref=src, dst_ref=dst, send_sem=sems.at[(0, *at)], recv_sem=sems.at[(1, *at)],
            device_id=to, device_id_type=MESH,
        )

    sends = []

    def send(src, dst, sems, at, to):
        copy = remote(src, dst, sems, at, to)
        copy.start()
        sends.append(copy)
        return copy

    def drain():
        for copy in sends:
            copy.wait_send()
        sends.clear()

    def behind(dx, dz):
        return lax.rem(x - dx + nx, nx) * nz + lax.rem(z - dz + nz, nz)

    def ahead(dx, dz):
        return lax.rem(x + dx, nx) * nz + lax.rem(z + dz, nz)

    def rows(brick, p):
        return pl.ds(pl.multiple_of(brick * columns + p * half, half), half)

    def block(brick):
        return pl.ds(pl.multiple_of(brick * columns, columns), columns)

    lanes = lax.broadcasted_iota(jnp.int32, (columns, columns), 1)

    for k in range(sources):
        id_cols[k] = ids_col[:, k : k + 1]
    acc[...] = jnp.zeros_like(acc)

    def pick_from(value, brick):
        th[...], tl[...] = split(value)

        def one(k, carry):
            at = pl.ds(pl.multiple_of(k * columns, columns), columns)
            pick = jnp.where(id_cols[k] - brick * columns == lanes, 1.0, 0.0).astype(BF16)
            acc[at, :] = acc[at, :] + (dot(pick, th[...]) + dot(pick, tl[...]))
            return carry

        lax.fori_loop(0, sources, one, 0)

    def take(brick):
        if in_vmem:
            pick_from(field[block(brick), :], brick)
        else:
            copy = pltpu.make_async_copy(field.at[block(brick), :], stage, local)
            copy.start()
            copy.wait()
            pick_from(stage[...], brick)

    def forward_stage(turn, between):
        source = est.at[at_half, :] if turn == 0 else mine

        def land(dx, dz, p):
            return field.at[rows(behind(dx, dz), p), :]

        def to_x(src, dz):
            for dx in range(1, nx):
                send(src, land(0, dz, parity), gx, (turn, dx, dz), peer_x(dx))

        def to_mate(src, dx, dz):
            send(src, land(dx, dz, parity), gm, (turn, dx, dz), {"view": mate})

        if turn > 0:
            keep = pltpu.make_async_copy(mine, land(0, 0, parity), local)
            keep.start()
            keep.wait()
            acc[...] = jnp.zeros_like(acc)

        def from_mate(dx, dz):
            remote(
                land(dx, dz, 1 - parity), land(dx, dz, 1 - parity), gm, (turn, dx, dz),
                {"view": mate},
            ).wait_recv()

        to_x(source, 0)
        for dz in range(nz - 1, 0, -1):
            send(source, land(0, 0, parity), gz, (turn, dz), peer_z(dz))
        if turn > 0:
            to_mate(source, 0, 0)
        between()
        here = behind(0, 0)
        if turn == 0:
            pick_from(est[...], here)
        else:
            from_mate(0, 0)
            take(here)
        waiting = []
        for dz in range(1, nz):
            remote(
                land(0, dz, parity), land(0, dz, parity), gz, (turn, dz), peer_z(dz)
            ).wait_recv()
            to_x(land(0, dz, parity), dz)
            to_mate(land(0, dz, parity), 0, dz)
            waiting.append((0, dz))
            if len(waiting) > 1:
                from_mate(*waiting[0])
                take(behind(*waiting.pop(0)))
        for dz in range(nz):
            for dx in range(1, nx):
                remote(
                    land(dx, dz, parity), land(dx, dz, parity), gx, (turn, dx, dz), peer_x(dx)
                ).wait_recv()
                to_mate(land(dx, dz, parity), dx, dz)
                waiting.append((dx, dz))
                from_mate(*waiting[0])
                take(behind(*waiting.pop(0)))
        for at in waiting:
            from_mate(*at)
            take(behind(*at))
        drain()

    def local_stage():
        own_rows = lambda k: pl.ds(pl.multiple_of(k * columns, columns), columns)

        def joined(k, forward):
            gh, gl = split(acc[own_rows(k), :])
            return forward + dot3(gh, gl, rh[k], rl[k])

        forward = lax.fori_loop(0, sources, joined, jnp.zeros((columns, depth), F32))
        fh, fl = split(forward)
        qh, ql = split(recorded[...] / dot3(fh, fl, bh[...], bl[...]))
        th[...], tl[...] = split(dot3(qh, ql, bth[...], btl[...]))

        def piece(k, carry):
            at = own_rows(k)
            ch[at, :], cl[at, :] = split(dot3(th[...], tl[...], rth[k], rtl[k]))
            return carry

        lax.fori_loop(0, sources, piece, 0)

    sub = lax.broadcasted_iota(jnp.int32, (columns, pairs), 0)

    def back_stage(turn, count_copies):
        from_x, from_z = {}, {}

        def produce(dx, dz):
            brick = ahead(dx, dz)
            put = jnp.where(ids_row[...] - brick * columns == sub, 1.0, 0.0).astype(BF16)
            partial[block(brick), :] = dot(put, ch[...]) + dot(put, cl[...])
            return send(
                partial.at[rows(brick, 1 - parity), :], mbuf.at[dx, dz], fm, (turn, dx, dz),
                {"view": mate},
            )

        def pass_on(dx, dz, copy):
            copy.wait_recv()
            total = mbuf[dx, dz] + partial[rows(ahead(dx, dz), parity), :]
            if dx:
                mbuf[dx, dz] = total
                from_x[dx, dz] = send(
                    mbuf.at[dx, dz], xbuf.at[dx, dz], fx, (turn, dx, dz), peer_x(dx)
                )
                return
            for d in range(1, nx):
                from_x[d, dz].wait_recv()
                total = total + xbuf[d, dz]
            if dz:
                mbuf[0, dz] = total
                from_z[dz] = send(mbuf.at[0, dz], zbuf.at[dz], fz, (turn, dz), peer_z(dz))
            else:
                own[...] = total

        order = [(dx, dz) for dx in range(nx - 1, -1, -1) for dz in range(nz - 1, -1, -1)]
        waiting = []
        for dx, dz in order:
            waiting.append((dx, dz, produce(dx, dz)))
            if len(waiting) > 1:
                pass_on(*waiting.pop(0))
        for item in waiting:
            pass_on(*item)
        for dz in range(nz - 1, 0, -1):
            from_z[dz].wait_recv()
            own[...] = own[...] + zbuf[dz]
        from_y = [
            send(own, ybuf.at[turn, j], fy, (turn, j), peer_v(2 * j)) for j in range(1, nv // 2)
        ]
        if turn == 0:
            for copy in count_copies:
                copy.wait_recv()
            summed = jnp.zeros((half, depth), F32)
            for w in range(nv):
                for k in range(sources):
                    summed = summed + cnt[w, at_half, k : k + 1] * units[w, k : k + 1, :]
            norm[...] = summed
        total = own[...]
        for j, copy in enumerate(from_y):
            copy.wait_recv()
            total = total + ybuf[turn, j + 1]
        drain()
        return total

    id_copies = []

    def first_work():
        for dx, dz in others:
            id_copies.append(
                send(ids_turned, idsbuf.at[dx, dz], isem, (dx, dz), peer_xz(dx, dz))
            )
        idsbuf[0, 0] = ids_turned[...]
        prep_stage(taps, r_ref, bh, bl, bth, btl, rh, rl, rth, rtl, my_unit)

    def count_ids():
        for copy in id_copies:
            copy.wait_recv()
        here = behind(0, 0) * columns
        inner = lax.broadcasted_iota(jnp.int32, (columns, columns), 0) + here
        slot = lax.broadcasted_iota(jnp.int32, (columns, 128), 1)
        counted = jnp.zeros((columns, 128), F32)
        for k in range(sources):
            hits = jnp.zeros((columns, columns), F32)
            for dx in range(nx):
                for dz in range(nz):
                    hits = hits + jnp.where(idsbuf[dx, dz, k : k + 1, :] == inner, 1.0, 0.0)
            counted = jnp.where(slot == k, jnp.sum(hits, axis=1, keepdims=True), counted)
        my_count[...] = counted
        cnt[v] = counted
        units[v] = my_unit[...]
        copies = []
        for d in range(1, nv):
            copies.append(send(my_count, cnt.at[v], csem, (d,), peer_v(d)))
            copies.append(send(my_unit, units.at[v], usem, (d,), peer_v(d)))
        return copies

    forward_stage(0, first_work)
    count_copies = count_ids()
    local_stage()
    total = back_stage(0, count_copies)
    for turn in range(1, ITERS):
        now = (est[at_half, :] if turn == 1 else mine[...]) * (total + 1.0) / (norm[...] + 1.0)
        mine[...] = now
        forward_stage(turn, lambda: None)
        local_stage()
        total = back_stage(turn, [])
    here = est[at_half, :] if ITERS == 1 else mine[...]
    out[at_half, :] = here * (total + 1.0) / (norm[...] + 1.0)
    last = remote(out.at[at_half, :], out.at[at_half, :], osem, (0,), {"view": mate})
    last.start()
    last.wait()


def per_device(estimate, recorded, resample, psf_taps, source_brick, source_column):
    nx, nz, nv = lax.axis_size("bx"), lax.axis_size("by"), lax.axis_size("view")
    columns, depth = estimate.shape
    sources = source_brick.shape[2]
    total, half, pairs = columns * nx * nz, columns // 2, columns * sources
    ids = source_brick[0] * columns + source_column[0]
    ids_turned = ids.T
    vm, smem = pl.BlockSpec(memory_space=VMEM), pl.BlockSpec(memory_space=pltpu.SMEM)
    in_vmem = total * depth * 4 <= 8 << 20
    out_shape = [jax.ShapeDtypeStruct((columns, depth), F32)]
    out_specs = [vm]
    scratch = []
    if in_vmem:
        scratch.append(VMEM((total, depth), F32))
    else:
        out_shape.append(jax.ShapeDtypeStruct((total, depth), F32))
        out_specs.append(pl.BlockSpec(memory_space=pl.ANY))
    dma = pltpu.SemaphoreType.DMA
    scratch += [
        VMEM((8 if in_vmem else columns, depth), F32),
        VMEM((half, depth), F32),
        VMEM((half, depth), F32),
        VMEM((columns, 128), F32),
        VMEM((sources, depth), F32),
        VMEM((half, depth), F32),
        VMEM((total, depth), F32),
        VMEM((nx, nz, half, depth), F32),
        VMEM((nx, nz, half, depth), F32),
        VMEM((nz, half, depth), F32),
        VMEM((ITERS, nv // 2, half, depth), F32),
        VMEM((nx, nz, sources, columns), jnp.int32),
        VMEM((nv, columns, 128), F32),
        VMEM((nv, sources, depth), F32),
    ]
    scratch += [VMEM((depth, depth), BF16)] * 4
    scratch += [VMEM((sources, depth, depth), BF16)] * 4
    scratch += [VMEM((pairs, depth), F32)] + [VMEM((pairs, depth), BF16)] * 2
    scratch += [VMEM((columns, depth), BF16)] * 2 + [VMEM((sources, columns, 1), jnp.int32)]
    scratch += [
        dma((2, ITERS, nz)), dma((2, ITERS, nx, nz)), dma((2, ITERS, nx, nz)),
        dma((2, ITERS, nz)), dma((2, ITERS, nx, nz)), dma((2, ITERS, nx, nz)),
        dma((2, ITERS, nv // 2)), dma((2, nx, nz)), dma((2, nv)), dma((2, nv)), dma((2, 1)), dma,
    ]
    return pl.pallas_call(
        kernel,
        out_shape=out_shape,
        in_specs=[smem] + [vm] * 6,
        out_specs=out_specs,
        scratch_shapes=scratch,
        compiler_params=pltpu.CompilerParams(
            collective_id=1, has_side_effects=True, vmem_limit_bytes=(48 if in_vmem else 62) << 20
        ),
        name="deconvolve",
    )(psf_taps, resample[0], estimate, recorded[0], ids, ids_turned.reshape(1, pairs), ids_turned)[0]


def solution(mesh):
    return jax.shard_map(
        per_device,
        mesh=mesh,
        in_specs=(
            P(("bx", "by"), None),
            P("view", ("bx", "by"), None),
            P("view", None, None, None),
            P("view", None),
            P("view", ("bx", "by"), None),
            P("view", ("bx", "by"), None),
        ),
        out_specs=P(("bx", "by"), None),
        check_vma=False,
    )
```

time: 903 us -> 192 us (0.21); the launches traced: 891 us -> 190 us
  blocking collectives: 307 us -> 0 us
  Pallas kernels: 0 us -> 184 us
  other arithmetic: 173 us -> 0.71 us
  local copies, waits for them, and re-layouts: 164 us -> 5.86 us
  matrix products: 126 us -> 0 us
  waiting for transfers between devices: 101 us -> 0 us
  between operations: 14 us -> 0.03 us
    all_to_all x4 -> x0, blocking collectives: 307 us -> none  [the longest x2 217 us: per_device(): lax.all_to_all(buffer.reshape(peer_count, capacity, layers, column_len),...]
    pallas_call x0 -> x1, Pallas kernels: none -> 184 us  [per_device(): pl.pallas_call(kernel, out_shape=out_shape, in_specs=[smem] + [vm] * 6, o...]
    scatter-add x2 -> x0, other arithmetic: 136 us -> none  [per_device(): jnp.zeros((columns, layers, column_len), jnp.float32).at[owned_column]]
    dot_general x9 -> x0, matrix products: 126 us -> none  [the longest x2 49.9 us: per_device(): smeared = jnp.dot(quotient, blurring.T, precision=precise)]
    scatter x3 -> x0, local copies, waits for them, and re-layouts: 116 us -> none  [the longest x2 112 us: per_device(): buffer = jnp.zeros((peer_count * capacity, layers, column_len), jnp.float...]
    psum x2 -> x0, waiting for transfers between devices: 64.2 us -> none  [per_device(): view_total = lax.psum(summands, 'view')]
    all_to_all x1 -> x0, waiting for transfers between devices: 37 us -> none  [per_device(): lax.all_to_all(outgoing.reshape(peer_count, capacity, column_len), ('bx',...]
    reduce_sum x3 -> x0, other arithmetic: 23.4 us -> none  [the longest x1 22.8 us: per_device(): unit_smeared = jnp.sum(blurring, axis=1)]
  transfers between devices with their start and end apart: 3 -> 0, of which waited for: 3 -> 0; matrix products, arithmetic and copies ran while one was open for 4% -> 0% of each run, Pallas kernels for 0% -> 0%
where the time goes in v2:
time: 192 us; the launch traced here: 190 us
  Pallas kernels  184 us (96%)
  local copies, waits for them, and re-layouts  5.86 us (3%)
    pallas_call x1, Pallas kernels, per_device(): pl.pallas_call(kernel, out_shape=out_shape, in_specs=[smem] + [vm] * 6, o...  184 us
    unnamed x10, local copies, waits for them, and re-layouts  5.73 us

profile of v2, /device:TPU:0, one launch (start us, length us, event | category | flops | bytes accessed | tf_op | source)
XLA Modules:
  0.0 190.5 jit_solution(4191858346509636998)
XLA Ops:
  0.0 0.7 fusion.1
  0.7 0.1 copy.7.ids_col
  0.9 0.0 copy-start
  0.9 2.2 %copy-done = f32[1,4,512,512]{3,2,1,0:T(8,128)S(1)} copy-done((f32[1,4,512,512]{3,2,1,0:T(8,128)S(1)}, f32[1,4,512,512]{3,2,1,0:T(8,128)}, u32[]{:S(2)}) %copy-start) | copy-done | bytes 4194328
  3.1 0.0 copy-start.1
  3.1 1.0 copy-done.1
  4.1 0.0 copy-start.2
  4.1 1.0 copy-done.2
  5.1 0.0 copy-start.3
  5.1 0.7 copy-done.3
  5.8 183.9 %deconvolve.1 = f32[256,512]{1,0:T(8,128)S(1)} custom-call(f32[1,31]{1,0:T(1,128)S(1)} %copy-done.3, f32[4,512,512]{2,1,0:T(8,128)S(1)} %bitcast.11, f32[256,512]{1,0:T(8,128)S(1)} %copy-done.1, f32[256,512]{1,0:T(8,128)S(1)} %bitcast.12, s32[256,4]{1,0:T(8,128)S(1)} %copy.7.ids_col, s32[1,1024]{1,0:T(1,128)S(1)} %bitcast.13, ...), custom_call_target="tpu_custom_call" | custom-call | tf_op jit(solution)/shard_map/deconvolve/pallas_call | solution.py:383
  189.7 0.8 copy.10
  (1 shorter events, 0.0 us)
Async XLA Ops:
  0.9 2.2 %copy-start = (f32[1,4,512,512]{3,2,1,0:T(8,128)S(1)}, f32[1,4,512,512]{3,2,1,0:T(8,128)}, u32[]{:S(2)}) copy-start(f32[1,4,512,512]{3,2,1,0:T(8,128)} %param.8) | copy-start | bytes 12582916
  3.1 1.0 copy-start.1
  4.1 1.0 copy-start.2
  5.1 0.7 copy-start.3

commit v3 on v2

--- a/solution.py
+++ b/solution.py
@@ -172,8 +172,13 @@
             ).wait_recv()
 
         to_x(source, 0)
-        for dz in range(nz - 1, 0, -1):
+        steps = sorted(range(1, nz), key=lambda d: min(d, nz - d))
+
+        def to_z(dz):
             send(source, land(0, 0, parity), gz, (turn, dz), peer_z(dz))
+
+        if nz > 1:
+            to_z(steps[0])
         if turn > 0:
             to_mate(source, 0, 0)
         between()
@@ -184,17 +189,19 @@
             from_mate(0, 0)
             take(here)
         waiting = []
-        for dz in range(1, nz):
+        for number, dz in enumerate(steps):
             remote(
                 land(0, dz, parity), land(0, dz, parity), gz, (turn, dz), peer_z(dz)
             ).wait_recv()
+            if number + 1 < len(steps):
+                to_z(steps[number + 1])
             to_x(land(0, dz, parity), dz)
             to_mate(land(0, dz, parity), 0, dz)
             waiting.append((0, dz))
             if len(waiting) > 1:
                 from_mate(*waiting[0])
                 take(behind(*waiting.pop(0)))
-        for dz in range(nz):
+        for dz in [0] + steps:
             for dx in range(1, nx):
                 remote(
                     land(dx, dz, parity), land(dx, dz, parity), gx, (turn, dx, dz), peer_x(dx)
@@ -259,7 +266,12 @@
             else:
                 own[...] = total
 
-        order = [(dx, dz) for dx in range(nx - 1, -1, -1) for dz in range(nz - 1, -1, -1)]
+        order = []
+        for dz in range(nz - 1, -1, -1):
+            order += [(dx, dz) for dx in range(nx - 1, 0, -1)]
+            if dz + 1 < nz:
+                order.append((0, dz + 1))
+        order.append((0, 0))
         waiting = []
         for dx, dz in order:
             waiting.append((dx, dz, produce(dx, dz)))

time: 192 us -> 185 us (0.964)
  the two profiles are of different devices: /device:TPU:0 before, /device:TPU:17 now
where the time goes in v3:
time: 185 us
  Pallas kernels  179 us (97%)
  local copies, waits for them, and re-layouts  5.86 us (3%)
    pallas_call x1, Pallas kernels, per_device(): pl.pallas_call(kernel, out_shape=out_shape, in_specs=[smem] + [vm] * 6, o...  179 us
    unnamed x10, local copies, waits for them, and re-layouts  5.73 us

profile of v3, /device:TPU:17, one launch (start us, length us, event | category | flops | bytes accessed | tf_op | source)
XLA Modules:
  0.0 185.2 jit_solution(4639811993305958237)
XLA Ops:
  0.0 0.7 fusion.1
  0.7 0.1 copy.7.ids_col
  0.9 0.0 copy-start
  0.9 2.2 %copy-done = f32[1,4,512,512]{3,2,1,0:T(8,128)S(1)} copy-done((f32[1,4,512,512]{3,2,1,0:T(8,128)S(1)}, f32[1,4,512,512]{3,2,1,0:T(8,128)}, u32[]{:S(2)}) %copy-start) | copy-done | bytes 4194328
  3.1 0.0 copy-start.1
  3.1 1.0 copy-done.1
  4.1 0.0 copy-start.2
  4.1 1.0 copy-done.2
  5.1 0.0 copy-start.3
  5.1 0.7 copy-done.3
  5.8 178.6 %deconvolve.1 = f32[256,512]{1,0:T(8,128)S(1)} custom-call(f32[1,31]{1,0:T(1,128)S(1)} %copy-done.3, f32[4,512,512]{2,1,0:T(8,128)S(1)} %bitcast.11, f32[256,512]{1,0:T(8,128)S(1)} %copy-done.1, f32[256,512]{1,0:T(8,128)S(1)} %bitcast.12, s32[256,4]{1,0:T(8,128)S(1)} %copy.7.ids_col, s32[1,1024]{1,0:T(1,128)S(1)} %bitcast.13, ...), custom_call_target="tpu_custom_call" | custom-call | tf_op jit(solution)/shard_map/deconvolve/pallas_call | solution.py:395
  184.4 0.8 copy.10
  (1 shorter events, 0.0 us)
Async XLA Ops:
  0.9 2.2 %copy-start = (f32[1,4,512,512]{3,2,1,0:T(8,128)S(1)}, f32[1,4,512,512]{3,2,1,0:T(8,128)}, u32[]{:S(2)}) copy-start(f32[1,4,512,512]{3,2,1,0:T(8,128)} %param.8) | copy-start | bytes 12582916
  3.1 1.0 copy-start.1
  4.1 1.0 copy-start.2
  5.1 0.7 copy-start.3
